TPU v7x, 256 devices: a whole 4x4x8 slice. The times are simulated.
256 devices in a mesh: row: 32 (over y, z), col: 8 (over x, core).
Axes of the slice: x: 4, y: 4, z: 8, core: 2. Of those that a mesh axis runs over, the one named last changes fastest.
Arguments:
- trail_adjoint: float32 [24576, 24576], P('row', 'col'), may hold values from -3 to 3
- panel: float32 [24576, 256], P(('row', 'col')), may hold values from -0.0390625 to 0.0390625
- panel_adjoint: float32 [24576, 256], P(('row', 'col')), may hold values from -6 to 6
- diag_factor: float32 [256, 256], replicated, as said below
- diag_inverse: float32 [256, 256], replicated, as said below
- diag_adjoint: float32 [256, 256], replicated, may hold values from -6 to 6
Outputs:
- panel_grad: float32 [24576, 256], P(('row', 'col'))
- diag_grad: float32 [256, 256], replicated
Inputs may be any that keep to these rules, and one draw needn't show every extreme that they name: diag_factor is lower triangular with a diagonal between 1 and 2, and diag_inverse is its inverse. diag_factor is lower triangular with a diagonal between 1 and 2.
All inputs are finite; a program needn't handle non-finite values.
Results may differ from a plain program's by a relative error of at most 0.000057.
Values sent between devices are 32-bit elements; how exact they have to be, the bound alone decides.
A program may use at most 128 MiB of HBM per device.

v0:
```python
import jax
import jax.numpy as jnp
from jax import lax
from jax.sharding import PartitionSpec as P


def lower_half(matrix):
    return jnp.tril(matrix) - 0.5 * jnp.diag(jnp.diag(matrix))


def on_device(trail_adjoint, panel, panel_adjoint, diag_factor, diag_inverse, diag_adjoint):
    highest = lax.Precision.HIGHEST
    col_place = lax.axis_index("col")
    trail_width = trail_adjoint.shape[1]
    row_block = lax.all_gather(panel, "col", axis=0, tiled=True)
    full_panel = lax.all_gather(row_block, "row", axis=0, tiled=True)
    column_panel = lax.dynamic_slice_in_dim(full_panel, col_place * trail_width, trail_width, 0)
    image = lax.psum_scatter(
        jnp.dot(trail_adjoint, column_panel, precision=highest, preferred_element_type=jnp.float32),
        "col",
        scatter_dimension=0,
        tiled=True,
    )
    updated = panel_adjoint - 2.0 * image
    panel_grad = jnp.dot(
        updated, diag_inverse, precision=highest, preferred_element_type=jnp.float32
    )
    local_gram = jnp.dot(panel_grad.T, panel, precision=highest, preferred_element_type=jnp.float32)
    gram = lax.psum(local_gram, ("row", "col"))
    corner = diag_adjoint - gram
    inner = lower_half(
        jnp.dot(diag_factor.T, corner, precision=highest, preferred_element_type=jnp.float32)
    )
    left_part = jnp.dot(
        diag_inverse.T, inner, precision=highest, preferred_element_type=jnp.float32
    )
    diag_grad = lower_half(
        jnp.dot(left_part, diag_inverse, precision=highest, preferred_element_type=jnp.float32)
    )
    return (panel_grad, diag_grad)


def solution(mesh):
    in_specs = (P("row", "col"), P(("row", "col"), None), P(("row", "col"), None), P(), P(), P())
    out_specs = (P(("row", "col"), None), P())
    return jax.shard_map(
        on_device, mesh=mesh, in_specs=in_specs, out_specs=out_specs, check_vma=False
    )
```

profile of v0, /device:TPU:2, one launch (start us, length us, event | category | flops | bytes accessed | tf_op | source)
XLA Modules:
  0.0 522.4 jit_solution(10304371956958443014)
XLA Ops:
  7.2 0.0 copy-start
  7.2 0.0 copy-start.1
  7.2 0.0 copy-start.5
  7.2 0.0 all-gather.2.cloned.1.call-start
  7.3 14.9 %all_gather.6 = f32[768,256]{1,0:T(8,128)} all-gather(f32[96,256]{1,0:T(8,128)} %param.7), channel_id=1, replica_groups=mesh['row'=32,'col'=8] {'col'}, dimensions={0}, use_global_device_ids=true | all-gather | bytes 884736 | tf_op jit(solution)/shard_map/all_gather | solution.py:15
  22.1 0.0 all-gather.2.cloned.1.call-update
  22.2 0.0 reduce-scatter.2.cloned.1.call-start
  22.2 186.5 %all-gather.2.cloned.1.call-done = f32[24576,256]{1,0:T(8,128)} async-done(((f32[768,256]{1,0:T(8,128)}), f32[24576,256]{1,0:T(8,128)}) %all-gather.2.cloned.1.call-update) | async-done | bytes 25165840 | tf_op jit(solution)/shard_map/all_gather | solution.py:16
  208.7 11.5 %fusion.2 = f32[768,256]{1,0:T(8,128)} fusion(f32[768,3072]{1,0:T(8,128)} %param.6, f32[24576,256]{1,0:T(8,128)} %all-gather.2.cloned.1.call-done, s32[]{:T(128)S(6)} %select_n.26), kind=kOutput, calls=%fused_computation.4 | convolution fusion | flops 7247757312 | bytes 13369348 | tf_op jit(solution)/shard_map/dot_general | solution.py:19
  220.2 0.0 reduce-scatter.2.cloned.1.call-update
  220.3 0.0 all-reduce.2.cloned.1.call-start
  220.3 28.0 %reduce-scatter.2.cloned.1.call-done = f32[96,256]{1,0:T(8,128)} async-done(((f32[768,256]{1,0:T(8,128)}), f32[96,256]{1,0:T(8,128)}) %reduce-scatter.2.cloned.1.call-update) | async-done | bytes 98320 | tf_op jit(solution)/shard_map/reduce_scatter | solution.py:18
  248.3 1.2 fusion.14
  249.5 0.0 copy-start.2
  249.5 1.1 fusion.22
  250.6 0.0 all-reduce.2.cloned.1.call-update
  250.6 256.9 %all-reduce.2.cloned.1.call-done = f32[256,256]{1,0:T(8,128)} async-done(((f32[256,256]{1,0:T(8,128)}), f32[256,256]{1,0:T(8,128)}) %all-reduce.2.cloned.1.call-update) | async-done | bytes 262160 | tf_op jit(solution)/shard_map/psum | solution.py:29
  507.6 1.5 convolution_bitcast_fusion
  509.2 2.4 gather_fusion
  511.5 0.4 fusion.5
  511.9 0.6 fusion.23
  512.5 0.1 copy.10
  512.7 2.3 gather_fusion.1
  515.1 0.8 copy.11
  (10 shorter events, 0.1 us)
Async XLA Ops:
  7.2 241.1 %copy-start = (f32[256,256]{1,0:T(8,128)S(1)}, f32[256,256]{1,0:T(8,128)}, u32[]{:S(2)}) copy-start(f32[256,256]{1,0:T(8,128)} %param.10) | copy-start | bytes 786436
  7.2 242.3 %copy-start.1 = (f32[96,256]{1,0:T(8,128)S(1)}, f32[96,256]{1,0:T(8,128)}, u32[]{:S(2)}) copy-start(f32[96,256]{1,0:T(8,128)} %param.7) | copy-start | bytes 294916
  7.2 241.1 %copy-start.5 = (f32[96,256]{1,0:T(8,128)S(1)}, f32[96,256]{1,0:T(8,128)}, u32[]{:S(2)}) copy-start(f32[96,256]{1,0:T(8,128)} %param.8) | copy-start | bytes 294916
  7.2 500.4 %copy-start.3 = (f32[256,256]{1,0:T(8,128)S(1)}, f32[256,256]{1,0:T(8,128)}, u32[]{:S(2)}) copy-start(f32[256,256]{1,0:T(8,128)} %param.9) | copy-start | bytes 786436
  7.2 500.4 %copy-start.4 = (f32[256,256]{1,0:T(8,128)S(1)}, f32[256,256]{1,0:T(8,128)}, u32[]{:S(2)}) copy-start(f32[256,256]{1,0:T(8,128)} %param.11) | copy-start | bytes 786436
  7.2 201.5 %all-gather.2.cloned.1.call-start = ((), (), s32[]{:S(2)}) async-start(), calls=%async_computation.1 | async-start | bytes 25952256 | tf_op jit(solution)/shard_map/all_gather | solution.py:16
  22.2 226.1 %reduce-scatter.2.cloned.1.call-start = ((), (), s32[]{:S(2)}) async-start(), calls=%async_computation.2 | async-start | bytes 884736 | tf_op jit(solution)/shard_map/reduce_scatter | solution.py:18
  220.3 287.3 %all-reduce.2.cloned.1.call-start = ((), (), s32[]{:S(2)}) async-start(), calls=%async_computation.3 | async-start | bytes 524288 | tf_op jit(solution)/shard_map/psum | solution.py:29
  249.5 266.4 %copy-start.2 = (f32[96,256]{1,0:T(8,128)}, f32[96,256]{1,0:T(8,128)S(1)}, u32[]{:S(2)}) copy-start(f32[96,256]{1,0:T(8,128)S(1)} %fusion.14) | copy-start | bytes 294916
Sparse Core Ops, SparseCore 0:
  22.3 186.4 all-gather.1
  220.4 27.8 reduce-scatter.1
  255.2 252.3 all-reduce.1
where the time goes:
time: 523 us; the launch traced here: 522 us
  waiting for transfers between devices  472 us (90%)
  matrix products  16.3 us (3%)
  blocking collectives  14.9 us (3%)
  between operations  13.9 us (3%)
  local copies, waits for them, and re-layouts  5.71 us (1%)
    psum x1, waiting for transfers between devices, on_device(): gram = lax.psum(local_gram, ('row', 'col'))  257 us
    all_gather x1, waiting for transfers between devices, on_device(): full_panel = lax.all_gather(row_block, 'row', axis=0, tiled=True)  187 us
    reduce_scatter x1, waiting for transfers between devices, on_device(): lax.psum_scatter(jnp.dot(trail_adjoint, column_panel, precision=highest,...  28 us
    all_gather x1, blocking collectives, on_device(): row_block = lax.all_gather(panel, 'col', axis=0, tiled=True)  14.9 us
    dot_general x1, matrix products, on_device(): jnp.dot(trail_adjoint, column_panel, precision=highest, preferred_element...  11.5 us
  transfers between devices with their start and end apart: 3, of which 3 were waited for; matrix products, arithmetic and copies ran while one was open for 0% of the time, Pallas kernels for 0%

commit v1 on v0

--- a/solution.py
+++ b/solution.py
@@ -13,7 +13,9 @@
     col_place = lax.axis_index("col")
     trail_width = trail_adjoint.shape[1]
     row_block = lax.all_gather(panel, "col", axis=0, tiled=True)
-    full_panel = lax.all_gather(row_block, "row", axis=0, tiled=True)
+    full_panel = jnp.concatenate(
+        lax.all_to_all(jnp.stack([row_block] * lax.axis_size("row")), "row", 0, 0), axis=0
+    )
     column_panel = lax.dynamic_slice_in_dim(full_panel, col_place * trail_width, trail_width, 0)
     image = lax.psum_scatter(
         jnp.dot(trail_adjoint, column_panel, precision=highest, preferred_element_type=jnp.float32),

time: 523 us -> 955 us (1.83)
  waiting for transfers between devices: 472 us -> 882 us
  starting transfers between devices: 0.12 us -> 11.7 us
  local copies, waits for them, and re-layouts: 5.71 us -> 16.9 us
    all_to_all x0 -> x1, waiting for transfers between devices: none -> 584 us  [on_device(): lax.all_to_all(jnp.stack([row_block] * lax.axis_size('row')), 'row', 0, 0)]
    all_gather x1 -> x0, waiting for transfers between devices: 187 us -> none  [on_device(): full_panel = lax.all_gather(row_block, 'row', axis=0, tiled=True)]
    reduce_scatter x1, waiting for transfers between devices: 28 us -> 40.5 us  [on_device(): lax.psum_scatter(jnp.dot(trail_adjoint, column_panel, precision=highest,...]
    all_to_all x0 -> x1, starting transfers between devices: none -> 11.6 us  [on_device(): lax.all_to_all(jnp.stack([row_block] * lax.axis_size('row')), 'row', 0, 0)]
    another operation x0 -> x1, local copies, waits for them, and re-layouts: none -> 11.1 us  [on_device(): jnp.stack([row_block] * lax.axis_size('row'))]
where the time goes in v1:
time: 955 us
  waiting for transfers between devices  882 us (92%)
  local copies, waits for them, and re-layouts  16.9 us (2%)
  matrix products  16.3 us (2%)
  between operations  14.2 us (1%)
  blocking collectives  13.9 us (1%)
  starting transfers between devices  11.7 us (1%)
    all_to_all x1, waiting for transfers between devices, on_device(): lax.all_to_all(jnp.stack([row_block] * lax.axis_size('row')), 'row', 0, 0)  584 us
    psum x1, waiting for transfers between devices, on_device(): gram = lax.psum(local_gram, ('row', 'col'))  257 us
    reduce_scatter x1, waiting for transfers between devices, on_device(): lax.psum_scatter(jnp.dot(trail_adjoint, column_panel, precision=highest,...  40.5 us
  transfers between devices with their start and end apart: 3, of which 3 were waited for; matrix products, arithmetic and copies ran while one was open for 0% of the time, Pallas kernels for 0%

profile of v1, /device:TPU:2, one launch (start us, length us, event | category | flops | bytes accessed | tf_op | source)
XLA Modules:
  0.0 954.6 jit_solution(1261486127587217623)
XLA Ops:
  7.2 0.0 copy-start
  7.2 13.9 %all_gather.3 = f32[768,256]{1,0:T(8,128)S(1)} all-gather(f32[96,256]{1,0:T(8,128)} %param.7), channel_id=1, replica_groups=mesh['row'=32,'col'=8] {'col'}, dimensions={0}, use_global_device_ids=true | all-gather | bytes 884736 | tf_op jit(solution)/shard_map/all_gather | solution.py:15
  21.1 11.1 %stack.2 = f32[32,768,256]{2,1,0:T(8,128)} broadcast(f32[768,256]{1,0:T(8,128)S(1)} %all_gather.3), dimensions={1,2} | broadcast | bytes 25952256 | tf_op jit(solution)/shard_map/stack | solution.py:17
  32.2 11.6 %all-to-all-start = ((f32[32,768,256]{2,1,0:T(8,128)}), f32[32,768,256]{2,1,0:T(8,128)}, u32[]{:S(2)}, u32[]{:S(2)}) async-start(f32[32,768,256]{2,1,0:T(8,128)} %stack.2), calls=%async_computation | async-start | bytes 50331648 | tf_op jit(solution)/shard_map/all_to_all | solution.py:17
  43.8 0.0 copy-start.5
  43.8 0.0 copy-start.4
  43.8 0.0 reduce-scatter.2.cloned.1.call-start
  43.9 584.2 %all-to-all-done = f32[32,768,256]{2,1,0:T(8,128)} async-done(((f32[32,768,256]{2,1,0:T(8,128)}), f32[32,768,256]{2,1,0:T(8,128)}, u32[]{:S(2)}, u32[]{:S(2)}) %all-to-all-start) | async-done | bytes 25165856 | tf_op jit(solution)/shard_map/all_to_all | solution.py:17
  628.1 11.5 %fusion.2 = f32[768,256]{1,0:T(8,128)} fusion(f32[768,3072]{1,0:T(8,128)} %param.6, f32[24576,256]{1,0:T(8,128)} %bitcast, s32[]{:T(128)S(6)} %select_n.26), kind=kOutput, calls=%fused_computation.4 | convolution fusion | flops 7247757312 | bytes 13369348 | tf_op jit(solution)/shard_map/dot_general | solution.py:21
  639.6 0.0 reduce-scatter.2.cloned.1.call-update
  639.7 0.0 all-reduce.2.cloned.1.call-start
  639.7 40.5 %reduce-scatter.2.cloned.1.call-done = f32[96,256]{1,0:T(8,128)} async-done(((f32[768,256]{1,0:T(8,128)}), f32[96,256]{1,0:T(8,128)}) %reduce-scatter.2.cloned.1.call-update) | async-done | bytes 98320 | tf_op jit(solution)/shard_map/reduce_scatter | solution.py:20
  680.2 1.2 fusion.14
  681.4 0.0 copy-start.2
  681.4 1.1 fusion.22
  682.5 0.0 all-reduce.2.cloned.1.call-update
  682.5 256.9 %all-reduce.2.cloned.1.call-done = f32[256,256]{1,0:T(8,128)} async-done(((f32[256,256]{1,0:T(8,128)}), f32[256,256]{1,0:T(8,128)}) %all-reduce.2.cloned.1.call-update) | async-done | bytes 262160 | tf_op jit(solution)/shard_map/psum | solution.py:31
  939.4 1.5 convolution_bitcast_fusion
  941.0 2.4 gather_fusion
  943.3 0.4 fusion.5
  943.7 0.6 fusion.23
  944.3 0.1 copy.10
  944.5 2.3 gather_fusion.1
  946.9 0.8 copy.11
  (10 shorter events, 0.1 us)
Async XLA Ops:
  7.2 673.0 %copy-start = (f32[256,256]{1,0:T(8,128)S(1)}, f32[256,256]{1,0:T(8,128)}, u32[]{:S(2)}) copy-start(f32[256,256]{1,0:T(8,128)} %param.10) | copy-start | bytes 786436
  32.2 595.9 %all-to-all-start = ((f32[32,768,256]{2,1,0:T(8,128)}), f32[32,768,256]{2,1,0:T(8,128)}, u32[]{:S(2)}, u32[]{:S(2)}) async-start(f32[32,768,256]{2,1,0:T(8,128)} %stack.2), calls=%async_computation | async-start | bytes 50331648 | tf_op jit(solution)/shard_map/all_to_all | solution.py:17
  43.8 636.4 %copy-start.5 = (f32[96,256]{1,0:T(8,128)S(1)}, f32[96,256]{1,0:T(8,128)}, u32[]{:S(2)}) copy-start(f32[96,256]{1,0:T(8,128)} %param.8) | copy-start | bytes 294916
  43.8 637.5 %copy-start.1 = (f32[96,256]{1,0:T(8,128)S(1)}, f32[96,256]{1,0:T(8,128)}, u32[]{:S(2)}) copy-start(f32[96,256]{1,0:T(8,128)} %param.7) | copy-start | bytes 294916
  43.8 895.6 %copy-start.3 = (f32[256,256]{1,0:T(8,128)S(1)}, f32[256,256]{1,0:T(8,128)}, u32[]{:S(2)}) copy-start(f32[256,256]{1,0:T(8,128)} %param.9) | copy-start | bytes 786436
  43.8 895.6 %copy-start.4 = (f32[256,256]{1,0:T(8,128)S(1)}, f32[256,256]{1,0:T(8,128)}, u32[]{:S(2)}) copy-start(f32[256,256]{1,0:T(8,128)} %param.11) | copy-start | bytes 786436
  43.8 636.3 %reduce-scatter.2.cloned.1.call-start = ((), (), s32[]{:S(2)}) async-start(), calls=%async_computation.2 | async-start | bytes 884736 | tf_op jit(solution)/shard_map/reduce_scatter | solution.py:20
  639.7 299.8 %all-reduce.2.cloned.1.call-start = ((), (), s32[]{:S(2)}) async-start(), calls=%async_computation.3 | async-start | bytes 524288 | tf_op jit(solution)/shard_map/psum | solution.py:31
  681.4 266.4 %copy-start.2 = (f32[96,256]{1,0:T(8,128)}, f32[96,256]{1,0:T(8,128)S(1)}, u32[]{:S(2)}) copy-start(f32[96,256]{1,0:T(8,128)S(1)} %fusion.14) | copy-start | bytes 294916
Sparse Core Ops, SparseCore 0:
  639.8 40.3 reduce-scatter.1
  687.1 252.2 all-reduce.1
